TPU v7x, 32 devices: a whole 2x2x4 slice. The times are simulated.
32 devices in a mesh: dp: 16 (over z, y, x), tensor: 2 (over core).
Axes of the slice: x: 2, y: 2, z: 4, core: 2. Of those that a mesh axis runs over, the one named last changes fastest.
Arguments:
- block_input: bfloat16 [3136, 512], P('dp'), may hold values from -6 to 6
- ln1_gain: float32 [512], replicated, may hold values from 0.1 to 1.9
- ln1_bias: float32 [512], replicated, may hold values from -3 to 3
- w_qkv: bfloat16 [3, 512, 512], P(None, None, 'tensor'), may hold values from -0.25 to 0.25
- qv_bias: float32 [2, 512], P(None, 'tensor'), may hold values from -3 to 3
- bias_table: float32 [169, 16], P(None, 'tensor'), may hold values from -4 to 4
- w_proj: bfloat16 [512, 512], P('tensor'), may hold values from -1 to 1
- proj_bias: float32 [512], replicated, may hold values from -3 to 3
- ln2_gain: float32 [512], replicated, may hold values from 0.1 to 1.9
- ln2_bias: float32 [512], replicated, may hold values from -3 to 3
- w_fc1: bfloat16 [512, 2048], P(None, 'tensor'), may hold values from -0.25 to 0.25
- fc1_bias: float32 [2048], P('tensor'), may hold values from -3 to 3
- w_fc2: bfloat16 [2048, 512], P('tensor'), may hold values from -0.1875 to 0.1875
- fc2_bias: float32 [512], replicated, may hold values from -3 to 3
- region_ids: int32 [4, 49], replicated, may hold values from 0 to 3
- rel_index: int32 [49, 49], replicated, may hold values from 0 to 168
- cotangent: bfloat16 [3136, 512], P('dp'), may hold values from -6 to 6
Outputs:
- block_output: float32 [3136, 512], P('dp')
- dx: float32 [3136, 512], P('dp')
- g_ln1_gain: float32 [512], replicated
- g_ln1_bias: float32 [512], replicated
- g_qkv: float32 [3, 512, 512], P(None, None, 'tensor')
- g_qv_bias: float32 [2, 512], P(None, 'tensor')
- g_table: float32 [169, 16], P(None, 'tensor')
- g_proj: float32 [512, 512], P('tensor')
- g_proj_bias: float32 [512], replicated
- g_ln2_gain: float32 [512], replicated
- g_ln2_bias: float32 [512], replicated
- g_fc1: float32 [512, 2048], P(None, 'tensor')
- g_fc1_bias: float32 [2048], P('tensor')
- g_fc2: float32 [2048, 512], P('tensor')
- g_fc2_bias: float32 [512], replicated
All inputs are finite; a program needn't handle non-finite values.
Results may differ from a plain program's by a relative error of at most 0.012.
Values sent between devices are 32-bit elements; how exact they have to be, the bound alone decides.
No kernel may reach another device: no remote copies, remote signals or barrier semaphores. Data moves between devices by JAX's collectives and lax.ppermute only.
A program may use at most 64 MiB of HBM per device.

v0:
```python
import jax
import jax.numpy as jnp
from jax import lax
from jax.sharding import PartitionSpec as P

SIDE = 14
WIN = 7
SHIFT = 3
NWIN = 4
WTOK = 49
TABLE = 169


def layer_stats(values, gain, bias):
    mean = jnp.mean(values, -1, keepdims=True)
    centred = values - mean
    var = jnp.mean(centred * centred, -1, keepdims=True)
    rstd = lax.rsqrt(var + 1e-05)
    nhat = centred * rstd
    return (nhat * gain + bias, nhat, rstd)


def layer_back(dout, nhat, rstd, gain):
    dnorm = dout * gain
    return rstd * (
        dnorm
        - jnp.mean(dnorm, -1, keepdims=True)
        - nhat * jnp.mean(dnorm * nhat, -1, keepdims=True)
    )


def to_windows(values, nimg):
    width = values.shape[-1]
    per = SIDE // WIN
    grid = values.reshape(nimg, SIDE, SIDE, width)
    grid = jnp.roll(grid, (-SHIFT, -SHIFT), (1, 2))
    grid = grid.reshape(nimg, per, WIN, per, WIN, width).transpose(0, 1, 3, 2, 4, 5)
    return grid.reshape(-1, width)


def from_windows(values, nimg):
    width = values.shape[-1]
    per = SIDE // WIN
    grid = values.reshape(nimg, per, per, WIN, WIN, width).transpose(0, 1, 3, 2, 4, 5)
    grid = grid.reshape(nimg, SIDE, SIDE, width)
    grid = jnp.roll(grid, (SHIFT, SHIFT), (1, 2))
    return grid.reshape(-1, width)


def gelu_value(u):
    return 0.5 * u * (1.0 + lax.erf(u * 0.7071067811865476))


def gelu_slope(u):
    return (
        0.5 * (1.0 + lax.erf(u * 0.7071067811865476))
        + u * jnp.exp(-0.5 * u * u) * 0.3989422804014327
    )


def inner(left, right):
    return lax.dot_general(
        left, right, (((0,), (0,)), ((), ())), preferred_element_type=jnp.float32
    )


def outer(left, right):
    return lax.dot_general(
        left, right, (((1,), (1,)), ((), ())), preferred_element_type=jnp.float32
    )


def mixed(form, left, right):
    return jnp.einsum(form, left, right, preferred_element_type=jnp.float32)


def body(
    block_input,
    ln1_gain,
    ln1_bias,
    w_qkv,
    qv_bias,
    bias_table,
    w_proj,
    proj_bias,
    ln2_gain,
    ln2_bias,
    w_fc1,
    fc1_bias,
    w_fc2,
    fc2_bias,
    region_ids,
    rel_index,
    cotangent,
):
    nimg = block_input.shape[0] // (SIDE * SIDE)
    heads = bias_table.shape[1]
    local_width = w_qkv.shape[2]
    hdim = local_width // heads
    scale = hdim ** (-0.5)
    shape5 = (nimg, NWIN, WTOK, heads, hdim)
    onehot = (rel_index.reshape(-1)[:, None] == lax.iota(jnp.int32, TABLE)[None, :]).astype(
        jnp.float32
    )
    bias = jnp.dot(onehot, bias_table, precision=lax.Precision.HIGHEST).T.reshape(heads, WTOK, WTOK)
    same = region_ids[:, :, None] == region_ids[:, None, :]
    mask = jnp.where(same, jnp.float32(0.0), jnp.float32(-100.0))
    xf = block_input.astype(jnp.float32)
    anorm, nhat1, rstd1 = layer_stats(xf, ln1_gain, ln1_bias)
    aw = to_windows(anorm.astype(jnp.bfloat16), nimg)
    query = (
        (jnp.dot(aw, w_qkv[0], preferred_element_type=jnp.float32) + qv_bias[0]) * scale
    ).astype(jnp.bfloat16)
    keys = jnp.dot(aw, w_qkv[1], preferred_element_type=jnp.float32).astype(jnp.bfloat16)
    values = (jnp.dot(aw, w_qkv[2], preferred_element_type=jnp.float32) + qv_bias[1]).astype(
        jnp.bfloat16
    )
    q5 = query.reshape(shape5)
    k5 = keys.reshape(shape5)
    v5 = values.reshape(shape5)
    scores = mixed("nwihd,nwjhd->nwhij", q5, k5) + bias[None, None] + mask[None, :, None]
    expo = jnp.exp(scores)
    total = jnp.sum(expo, -1, keepdims=True)
    probs = expo / total
    lse = jnp.log(total)
    attn5 = mixed("nwhij,nwjhd->nwihd", probs.astype(jnp.bfloat16), v5).astype(jnp.bfloat16)
    attn_flat = attn5.reshape(-1, local_width)
    projected = lax.psum(jnp.dot(attn_flat, w_proj, preferred_element_type=jnp.float32), "tensor")
    hres = xf + from_windows(projected, nimg) + proj_bias
    cnorm, nhat2, rstd2 = layer_stats(hres, ln2_gain, ln2_bias)
    cb = cnorm.astype(jnp.bfloat16)
    upre = jnp.dot(cb, w_fc1, preferred_element_type=jnp.float32) + fc1_bias
    zact = gelu_value(upre).astype(jnp.bfloat16)
    mlp_out = lax.psum(jnp.dot(zact, w_fc2, preferred_element_type=jnp.float32), "tensor")
    block_output = hres + mlp_out + fc2_bias
    gf = cotangent.astype(jnp.float32)
    g_fc2_bias = jnp.sum(gf, 0)
    g_fc2 = inner(zact, cotangent)
    du = outer(cotangent, w_fc2) * gelu_slope(upre)
    g_fc1_bias = jnp.sum(du, 0)
    dub = du.astype(jnp.bfloat16)
    g_fc1 = inner(cb, dub)
    dcn = lax.psum(outer(dub, w_fc1), "tensor")
    g_ln2_gain = jnp.sum(dcn * nhat2, 0)
    g_ln2_bias = jnp.sum(dcn, 0)
    dh = gf + layer_back(dcn, nhat2, rstd2, ln2_gain)
    g_proj_bias = jnp.sum(dh, 0)
    dhw = to_windows(dh, nimg).astype(jnp.bfloat16)
    g_proj = inner(attn_flat, dhw)
    dout = outer(dhw, w_proj).astype(jnp.bfloat16)
    d5 = dout.reshape(shape5)
    scores = mixed("nwihd,nwjhd->nwhij", q5, k5) + bias[None, None] + mask[None, :, None]
    probs = jnp.exp(scores - lse)
    pb = probs.astype(jnp.bfloat16)
    dprob = mixed("nwihd,nwjhd->nwhij", d5, v5)
    delta = jnp.sum(d5.astype(jnp.float32) * attn5.astype(jnp.float32), -1).transpose(0, 1, 3, 2)[
        ..., None
    ]
    dscore = probs * (dprob - delta)
    dv = mixed("nwhij,nwihd->nwjhd", pb, d5).reshape(-1, local_width)
    dbias = jnp.sum(dscore, (0, 1)).reshape(heads, WTOK * WTOK)
    g_table = lax.dot_general(
        onehot, dbias, (((0,), (1,)), ((), ())), precision=lax.Precision.HIGHEST
    )
    dsb = dscore.astype(jnp.bfloat16)
    dq = (mixed("nwhij,nwjhd->nwihd", dsb, k5) * scale).reshape(-1, local_width)
    dk = mixed("nwhij,nwihd->nwjhd", dsb, q5).reshape(-1, local_width)
    g_qv_bias = jnp.stack([jnp.sum(dq, 0), jnp.sum(dv, 0)])
    dqb = dq.astype(jnp.bfloat16)
    dkb = dk.astype(jnp.bfloat16)
    dvb = dv.astype(jnp.bfloat16)
    g_qkv = jnp.stack([inner(aw, dqb), inner(aw, dkb), inner(aw, dvb)])
    daw = outer(dqb, w_qkv[0]) + outer(dkb, w_qkv[1]) + outer(dvb, w_qkv[2])
    dan = lax.psum(from_windows(daw, nimg), "tensor")
    g_ln1_gain = jnp.sum(dan * nhat1, 0)
    g_ln1_bias = jnp.sum(dan, 0)
    dx = dh + layer_back(dan, nhat1, rstd1, ln1_gain)
    (
        g_ln1_gain,
        g_ln1_bias,
        g_qkv,
        g_qv_bias,
        g_table,
        g_proj,
        g_proj_bias,
        g_ln2_gain,
        g_ln2_bias,
        g_fc1,
        g_fc1_bias,
        g_fc2,
        g_fc2_bias,
    ) = lax.psum(
        (
            g_ln1_gain,
            g_ln1_bias,
            g_qkv,
            g_qv_bias,
            g_table,
            g_proj,
            g_proj_bias,
            g_ln2_gain,
            g_ln2_bias,
            g_fc1,
            g_fc1_bias,
            g_fc2,
            g_fc2_bias,
        ),
        "dp",
    )
    return (
        block_output,
        dx,
        g_ln1_gain,
        g_ln1_bias,
        g_qkv,
        g_qv_bias,
        g_table,
        g_proj,
        g_proj_bias,
        g_ln2_gain,
        g_ln2_bias,
        g_fc1,
        g_fc1_bias,
        g_fc2,
        g_fc2_bias,
    )


def solution(mesh):
    return jax.shard_map(
        body,
        mesh=mesh,
        in_specs=(
            P("dp", None),
            P(),
            P(),
            P(None, None, "tensor"),
            P(None, "tensor"),
            P(None, "tensor"),
            P("tensor", None),
            P(),
            P(),
            P(),
            P(None, "tensor"),
            P("tensor"),
            P("tensor", None),
            P(),
            P(),
            P(),
            P("dp", None),
        ),
        out_specs=(
            P("dp", None),
            P("dp", None),
            P(),
            P(),
            P(None, None, "tensor"),
            P(None, "tensor"),
            P(None, "tensor"),
            P("tensor", None),
            P(),
            P(),
            P(),
            P(None, "tensor"),
            P("tensor"),
            P("tensor", None),
            P(),
        ),
        check_vma=False,
    )
```

profile of v0, /device:TPU:0, one launch (start us, length us, event | category | flops | bytes accessed | tf_op | source)
XLA Modules:
  0.0 377.0 jit_solution(15921145427322588425)
XLA Ops:
  13.9 1.9 convolution_bitcast_fusion
  27.3 2.2 copy.85
  29.6 21.2 %all-reduce.8.cloned.1.call-done = f32[1,14,14,512]{3,0,2,1:T(1,128)} async-done(((f32[1,14,14,512]{3,0,2,1:T(1,128)}), f32[1,14,14,512]{3,0,2,1:T(1,128)}) %all-reduce.8.cloned.1.call-update) | async-done | bytes 401424 | tf_op jit(solution)/shard_map/psum | solution.py:128
  52.9 1.8 fusion.38
  60.6 2.4 fusion.68
  63.0 1.9 fusion.55
  64.9 15.3 %all-reduce.10.cloned.1.call-done = f32[196,512]{1,0:T(8,128)} async-done(((f32[196,512]{1,0:T(8,128)}), f32[196,512]{1,0:T(8,128)}) %all-reduce.10.cloned.1.call-update) | async-done | bytes 401424 | tf_op jit(solution)/shard_map/psum | solution.py:143
  80.2 1.9 multiply_reduce_fusion.1
  82.0 2.6 fusion.59
  84.7 1.7 reshape.241
  92.3 1.7 convert_element_type.127
  94.0 1.9 convolution_convert_fusion.2
  95.9 1.9 reshape.252
  97.8 2.0 reshape.248
  99.9 2.0 copy.88
  101.8 2.3 copy.91
  112.1 1.9 copy.98
  115.1 1.9 copy.95
  122.6 1.8 fusion.70
  129.7 13.3 %all-reduce.14.cloned.1.call-done = (f32[196,512]{1,0:T(8,128)}, f32[196,512]{1,0:T(8,128)}) async-done(((f32[196,512]{1,0:T(8,128)}, f32[196,512]{1,0:T(8,128)}), (f32[196,512]{1,0:T(8,128)}, f32[196,512]{1,0:T(8,128)})) %all-reduce.14.cloned.1.call-update) | async-done | bytes 802832 | tf_op jit(solution)/shard_map/psum | solution.py:134
  144.5 80.1 %all-reduce = (f32[512]{0:T(512)}, f32[512]{0:T(512)}, f32[2,256]{1,0:T(2,128)}, f32[169,8]{0,1:T(8,128)}, f32[512]{0:T(512)}, /*index=5*/f32[512]{0:T(512)}, f32[512]{0:T(512)}, f32[1024]{0:T(1024)}, f32[512]{0:T(512)}) all-reduce(f32[512]{0:T(512)S(1)} %get-tuple-element.17, ...), channel_id=1, replica_groups=mesh['dp'=16,'tensor'=2] {'dp'}, use_global_device_ids=true, to_apply=%region_15.16 | all-reduce | flops 5960 | bytes 47680 | tf_op jit(solution)/shard_map/psum | solution.py:192
  224.5 1.8 add_add_fusion
  227.3 135.8 %all-reduce.12.cloned.1.call-done = (f32[3,512,256]{2,1,0:T(8,128)}, f32[256,512]{1,0:T(8,128)}, f32[512,1024]{1,0:T(8,128)}, f32[1024,512]{1,0:T(8,128)}) async-done(((f32[3,512,256]{2,1,0:T(8,128)}, f32[256,512]{1,0:T(8,128)}, f32[512,1024]{1,0:T(8,128)}, f32[1024,512]{1,0:T(8,128)}), (f32[3,512,256]{2,1,0:T(8,128)}, f32[256,512]{1,0:T(8,128)}, f32[512,1024]{1,0:T(8,128)}, ...) | async-done | bytes 6291472 | tf_op jit(solution)/shard_map/psum | solution.py:192
  363.1 2.8 copy.129
  (171 shorter events, 58.3 us)
Async XLA Ops:
  7.2 49.1 %copy-start = (bf16[512,1024]{1,0:T(8,128)(2,1)S(1)}, bf16[512,1024]{1,0:T(8,128)(2,1)}, u32[]{:S(2)}) copy-start(bf16[512,1024]{1,0:T(8,128)(2,1)} %param.27) | copy-start | bytes 3145732
  7.2 43.6 %all-reduce.8.cloned.1.call-start = ((), (), s32[]{:S(2)}) async-start(), calls=%async_computation | async-start | bytes 802816 | tf_op jit(solution)/shard_map/psum | solution.py:128
  10.8 6.4 %copy-start.12 = (bf16[3,512,256]{2,1,0:T(8,128)(2,1)S(1)}, bf16[3,512,256]{2,1,0:T(8,128)(2,1)}, u32[]{:S(2)}) copy-start(bf16[3,512,256]{2,1,0:T(8,128)(2,1)} %param.20) | copy-start | bytes 2359300
  21.7 4.1 %copy-start.17 = (bf16[256,512]{1,0:T(8,128)(2,1)S(1)}, bf16[256,512]{1,0:T(8,128)(2,1)}, u32[]{:S(2)}) copy-start(bf16[256,512]{1,0:T(8,128)(2,1)} %param.23) | copy-start | bytes 786436
  27.3 28.5 %copy-start.1 = (bf16[196,512]{1,0:T(8,128)(2,1)S(1)}, bf16[196,512]{1,0:T(8,128)(2,1)}, u32[]{:S(2)}) copy-start(bf16[196,512]{1,0:T(8,128)(2,1)} %param.17) | copy-start | bytes 602116
  27.3 28.5 %copy-start.36 = (f32[512]{0:T(512)S(1)}, f32[512]{0:T(512)}, u32[]{:S(2)}) copy-start(f32[512]{0:T(512)} %param.24) | copy-start | bytes 6148
  29.5 26.7 %copy-start.25 = (f32[512]{0:T(512)S(1)}, f32[512]{0:T(512)}, u32[]{:S(2)}) copy-start(f32[512]{0:T(512)} %param.25) | copy-start | bytes 6148
  29.6 26.7 %copy-start.29 = (f32[512]{0:T(512)S(1)}, f32[512]{0:T(512)}, u32[]{:S(2)}) copy-start(f32[512]{0:T(512)} %param.26) | copy-start | bytes 6148
  29.6 26.7 %copy-start.34 = (f32[1024]{0:T(1024)S(1)}, f32[1024]{0:T(1024)}, u32[]{:S(2)}) copy-start(f32[1024]{0:T(1024)} %param.28) | copy-start | bytes 12292
  29.6 50.6 %all-reduce.10.cloned.1.call-start = ((), (), s32[]{:S(2)}) async-start(), calls=%async_computation.1 | async-start | bytes 819200 | tf_op jit(solution)/shard_map/psum | solution.py:143
  60.3 82.7 %all-reduce.14.cloned.1.call-start = ((), (), s32[]{:S(2)}) async-start(), calls=%async_computation.3 | async-start | bytes 1638400 | tf_op jit(solution)/shard_map/psum | solution.py:134
  104.1 3.9 %copy-start.4 = (bf16[4,49,8,32]{1,3,2,0:T(8,128)(2,1)S(1)}, bf16[4,49,8,32]{1,3,2,0:T(8,128)(2,1)}, u32[]{:S(2)}) copy-start(bf16[4,49,8,32]{1,3,2,0:T(8,128)(2,1)} %copy-done.3) | copy-start | bytes 301060
  109.0 9.1 %copy-start.13 = (bf16[3,512,256]{2,1,0:T(8,128)(2,1)S(1)}, bf16[3,512,256]{2,1,0:T(8,128)(2,1)}, u32[]{:S(2)}) copy-start(bf16[3,512,256]{2,1,0:T(8,128)(2,1)} %param.20) | copy-start | bytes 2359300
  122.5 240.6 %all-reduce.12.cloned.1.call-start = ((), (), s32[]{:S(2)}) async-start(), calls=%async_computation.2 | async-start | bytes 12582912 | tf_op jit(solution)/shard_map/psum | solution.py:192
  127.5 15.5 %copy-start.26 = (f32[512]{0:T(512)S(1)}, f32[512]{0:T(512)}, u32[]{:S(2)}) copy-start(f32[512]{0:T(512)} %param.18) | copy-start | bytes 6148
  127.5 16.9 %copy-start.30 = (f32[512]{0:T(512)S(1)}, f32[512]{0:T(512)}, u32[]{:S(2)}) copy-start(f32[512]{0:T(512)} %get-tuple-element.15) | copy-start | bytes 6148
  127.5 16.9 %copy-start.31 = (f32[512]{0:T(512)S(1)}, f32[512]{0:T(512)}, u32[]{:S(2)}) copy-start(f32[512]{0:T(512)} %get-tuple-element.21) | copy-start | bytes 6148
  127.5 16.9 %copy-start.32 = (f32[512]{0:T(512)S(1)}, f32[512]{0:T(512)}, u32[]{:S(2)}) copy-start(f32[512]{0:T(512)} %get-tuple-element.38) | copy-start | bytes 6148
  127.5 16.9 %copy-start.33 = (f32[512]{0:T(512)S(1)}, f32[512]{0:T(512)}, u32[]{:S(2)}) copy-start(f32[512]{0:T(512)} %get-tuple-element.46) | copy-start | bytes 6148
  127.6 16.9 %copy-start.35 = (f32[1024]{0:T(1024)S(1)}, f32[1024]{0:T(1024)}, u32[]{:S(2)}) copy-start(f32[1024]{0:T(1024)} %get-tuple-element.57) | copy-start | bytes 12292
  127.6 96.9 %copy-start.37 = (f32[512]{0:T(512)S(1)}, f32[512]{0:T(512)}, u32[]{:S(2)}) copy-start(f32[512]{0:T(512)} %param.30) | copy-start | bytes 6148
  127.6 98.7 %copy-start.2 = (f32[196,512]{1,0:T(8,128)S(1)}, f32[196,512]{1,0:T(8,128)}, u32[]{:S(2)}) copy-start(f32[196,512]{1,0:T(8,128)} %get-tuple-element.39) | copy-start | bytes 1204228
  143.0 83.3 %copy-start.11 = (f32[196,512]{1,0:T(8,128)S(1)}, f32[196,512]{1,0:T(8,128)}, u32[]{:S(2)}) copy-start(f32[196,512]{1,0:T(8,128)} %get-tuple-element.37) | copy-start | bytes 1204228
  363.1 3.6 copy-start.7
  (18 other events, 32.5 us)
Sparse Core Ops, SparseCore 0:
  29.7 21.1 all-reduce.7
  60.5 19.6 all-reduce.9
  122.6 20.3 all-reduce.13
  150.5 212.6 all-reduce.11
where the time goes:
time: 378 us; the launch traced here: 377 us
  waiting for transfers between devices  186 us (49%)
  blocking collectives  80.1 us (21%)
  local copies, waits for them, and re-layouts  50.5 us (13%)
  matrix products  25.6 us (7%)
  other arithmetic  20.3 us (5%)
  between operations  14.5 us (4%)
    psum x1, waiting for transfers between devices, body(): lax.psum((g_ln1_gain, g_ln1_bias, g_qkv, g_qv_bias, g_table, g_proj, g_pr...  136 us
    psum x1, blocking collectives, body(): lax.psum((g_ln1_gain, g_ln1_bias, g_qkv, g_qv_bias, g_table, g_proj, g_pr...  80.1 us
    psum x1, waiting for transfers between devices, body(): lax.psum(jnp.dot(attn_flat, w_proj, preferred_element_type=jnp.float32),...  21.2 us
    psum x1, waiting for transfers between devices, body(): dcn = lax.psum(outer(dub, w_fc1), 'tensor')  15.3 us
    psum x1, waiting for transfers between devices, body(): lax.psum(jnp.dot(zact, w_fc2, preferred_element_type=jnp.float32), 'tensor')  13.3 us
    unnamed x80, local copies, waits for them, and re-layouts  10.4 us
  transfers between devices with their start and end apart: 4, of which 4 were waited for; matrix products, arithmetic and copies ran while one was open for 4% of the time, Pallas kernels for 0%

commit v1 on v0

--- a/solution.py
+++ b/solution.py
@@ -9,6 +9,10 @@
 NWIN = 4
 WTOK = 49
 TABLE = 169
+
+
+def watch_view(mine_x, dev_axis):
+    return jnp.sum(jax.lax.all_gather(mine_x, dev_axis), axis=0)
 
 
 def layer_stats(values, gain, bias):
@@ -131,7 +135,7 @@
     cb = cnorm.astype(jnp.bfloat16)
     upre = jnp.dot(cb, w_fc1, preferred_element_type=jnp.float32) + fc1_bias
     zact = gelu_value(upre).astype(jnp.bfloat16)
-    mlp_out = lax.psum(jnp.dot(zact, w_fc2, preferred_element_type=jnp.float32), "tensor")
+    mlp_out = watch_view(jnp.dot(zact, w_fc2, preferred_element_type=jnp.float32), "tensor")
     block_output = hres + mlp_out + fc2_bias
     gf = cotangent.astype(jnp.float32)
     g_fc2_bias = jnp.sum(gf, 0)

time: 378 us -> 364 us (0.963)
  local copies, waits for them, and re-layouts: 50.5 us -> 34.9 us
  blocking collectives: 80.1 us -> 87 us
  waiting for transfers between devices: 186 us -> 181 us
    all_gather x0 -> x1, blocking collectives: none -> 6.94 us  [watch_view(): return jnp.sum(jax.lax.all_gather(mine_x, dev_axis), axis=0)]
    psum x1, waiting for transfers between devices: 15.3 us -> 8.93 us  [body(): dcn = lax.psum(outer(dub, w_fc1), 'tensor')]
    unnamed x80 -> x76, local copies, waits for them, and re-layouts: 10.4 us -> 9.93 us
  transfers between devices with their start and end apart: 4 -> 4, of which waited for: 4 -> 4; matrix products, arithmetic and copies ran while one was open for 4% -> 3% of each run, Pallas kernels for 0% -> 0%
where the time goes in v1:
time: 364 us; the launch traced here: 363 us
  waiting for transfers between devices  181 us (50%)
  blocking collectives  87 us (24%)
  local copies, waits for them, and re-layouts  34.9 us (10%)
  matrix products  23.8 us (7%)
  other arithmetic  21.7 us (6%)
  between operations  14.5 us (4%)
    psum x1, waiting for transfers between devices, body(): lax.psum((g_ln1_gain, g_ln1_bias, g_qkv, g_qv_bias, g_table, g_proj, g_pr...  137 us
    psum x1, blocking collectives, body(): lax.psum((g_ln1_gain, g_ln1_bias, g_qkv, g_qv_bias, g_table, g_proj, g_pr...  80 us
    psum x1, waiting for transfers between devices, body(): lax.psum(jnp.dot(attn_flat, w_proj, preferred_element_type=jnp.float32),...  21.2 us
    psum x1, waiting for transfers between devices, body(): dan = lax.psum(from_windows(daw, nimg), 'tensor')  14.1 us
    unnamed x76, local copies, waits for them, and re-layouts  9.93 us
    psum x1, waiting for transfers between devices, body(): dcn = lax.psum(outer(dub, w_fc1), 'tensor')  8.93 us
    dot_general x6, matrix products, inner(): lax.dot_general(left, right, (((0,), (0,)), ((), ())), preferred_element_...  7.37 us
  transfers between devices with their start and end apart: 4, of which 4 were waited for; matrix products, arithmetic and copies ran while one was open for 3% of the time, Pallas kernels for 0%

profile of v1, /device:TPU:0, one launch (start us, length us, event | category | flops | bytes accessed | tf_op | source)
XLA Modules:
  0.0 363.1 jit_solution(11654969663080202707)
XLA Ops:
  13.3 1.9 convolution_bitcast_fusion
  19.4 1.3 fusion.6
  25.5 21.2 %all-reduce.7.cloned.1.call-done = f32[1,14,14,512]{3,0,2,1:T(1,128)} async-done(((f32[1,14,14,512]{3,0,2,1:T(1,128)}), f32[1,14,14,512]{3,0,2,1:T(1,128)}) %all-reduce.7.cloned.1.call-update) | async-done | bytes 401424 | tf_op jit(solution)/shard_map/psum | solution.py:132
  52.8 1.8 fusion.69
  57.1 6.9 %all-gather.1 = f32[2,196,512]{2,1,0:T(8,128)} all-gather(f32[1,196,512]{2,1,0:T(8,128)} %convolution_bitcast_fusion.5), channel_id=2, replica_groups=mesh['dp'=16,'tensor'=2] {'tensor'}, dimensions={0}, use_global_device_ids=true | all-gather | bytes 1204224 | tf_op jit(solution)/shard_map/all_gather | solution.py:15
  64.0 2.0 reduce_sum.196
  66.0 1.9 fusion.55
  68.0 8.9 %all-reduce.9.cloned.1.call-done = f32[196,512]{1,0:T(8,128)} async-done(((f32[196,512]{1,0:T(8,128)}), f32[196,512]{1,0:T(8,128)}) %all-reduce.9.cloned.1.call-update) | async-done | bytes 401424 | tf_op jit(solution)/shard_map/psum | solution.py:147
  76.9 1.9 multiply_reduce_fusion.1
  78.8 2.8 fusion.59
  86.1 1.9 reshape.256
  88.0 2.0 reshape.252
  90.0 1.3 copy.88
  91.3 2.3 copy.91
  105.7 1.8 fusion.36
  107.5 1.8 reshape.245
  115.1 14.1 %all-reduce.11.cloned.1.call-done = f32[196,512]{1,0:T(8,128)} async-done(((f32[196,512]{1,0:T(8,128)}), f32[196,512]{1,0:T(8,128)}) %all-reduce.11.cloned.1.call-update) | async-done | bytes 401424 | tf_op jit(solution)/shard_map/psum | solution.py:178
  129.2 1.3 fusion.32
  130.5 80.0 %all-reduce = (f32[512]{0:T(512)}, f32[512]{0:T(512)}, f32[2,256]{1,0:T(2,128)}, f32[169,8]{0,1:T(8,128)}, f32[512]{0:T(512)}, /*index=5*/f32[512]{0:T(512)}, f32[512]{0:T(512)}, f32[1024]{0:T(1024)}, f32[512]{0:T(512)}) all-reduce(f32[512]{0:T(512)S(1)} %get-tuple-element.17, ...), channel_id=1, replica_groups=mesh['dp'=16,'tensor'=2] {'dp'}, use_global_device_ids=true, to_apply=%region_15.16 | all-reduce | flops 5960 | bytes 47680 | tf_op jit(solution)/shard_map/psum | solution.py:196
  210.5 1.9 fusion.31
  212.5 136.8 %all-reduce.13.cloned.1.call-done = (f32[3,512,256]{2,1,0:T(8,128)}, f32[256,512]{1,0:T(8,128)}, f32[512,1024]{1,0:T(8,128)}, f32[1024,512]{1,0:T(8,128)}) async-done(((f32[3,512,256]{2,1,0:T(8,128)}, f32[256,512]{1,0:T(8,128)}, f32[512,1024]{1,0:T(8,128)}, f32[1024,512]{1,0:T(8,128)}), (f32[3,512,256]{2,1,0:T(8,128)}, f32[256,512]{1,0:T(8,128)}, f32[512,1024]{1,0:T(8,128)}, ...) | async-done | bytes 6291472 | tf_op jit(solution)/shard_map/psum | solution.py:196
  349.3 2.8 copy.128
  352.9 1.3 copy.130
  355.2 1.3 copy.131
  (168 shorter events, 47.1 us)
Async XLA Ops:
  7.2 43.9 %copy-start = (bf16[512,1024]{1,0:T(8,128)(2,1)S(1)}, bf16[512,1024]{1,0:T(8,128)(2,1)}, u32[]{:S(2)}) copy-start(bf16[512,1024]{1,0:T(8,128)(2,1)} %param.27) | copy-start | bytes 3145732
  7.2 39.5 %all-reduce.7.cloned.1.call-start = ((), (), s32[]{:S(2)}) async-start(), calls=%async_computation | async-start | bytes 802816 | tf_op jit(solution)/shard_map/psum | solution.py:132
  10.8 5.1 %copy-start.6 = (bf16[3,512,256]{2,1,0:T(8,128)(2,1)S(1)}, bf16[3,512,256]{2,1,0:T(8,128)(2,1)}, u32[]{:S(2)}) copy-start(bf16[3,512,256]{2,1,0:T(8,128)(2,1)} %param.20) | copy-start | bytes 2359300
  12.4 3.1 copy-start.26
  19.4 4.1 %copy-start.13 = (bf16[256,512]{1,0:T(8,128)(2,1)S(1)}, bf16[256,512]{1,0:T(8,128)(2,1)}, u32[]{:S(2)}) copy-start(bf16[256,512]{1,0:T(8,128)(2,1)} %param.23) | copy-start | bytes 786436
  24.2 25.7 %copy-start.1 = (bf16[196,512]{1,0:T(8,128)(2,1)S(1)}, bf16[196,512]{1,0:T(8,128)(2,1)}, u32[]{:S(2)}) copy-start(bf16[196,512]{1,0:T(8,128)(2,1)} %param.17) | copy-start | bytes 602116
  25.4 25.7 %copy-start.20 = (f32[512]{0:T(512)S(1)}, f32[512]{0:T(512)}, u32[]{:S(2)}) copy-start(f32[512]{0:T(512)} %param.25) | copy-start | bytes 6148
  25.4 25.7 %copy-start.28 = (f32[512]{0:T(512)S(1)}, f32[512]{0:T(512)}, u32[]{:S(2)}) copy-start(f32[512]{0:T(512)} %param.26) | copy-start | bytes 6148
  25.4 25.7 %copy-start.33 = (f32[1024]{0:T(1024)S(1)}, f32[1024]{0:T(1024)}, u32[]{:S(2)}) copy-start(f32[1024]{0:T(1024)} %param.28) | copy-start | bytes 12292
  25.4 51.5 %all-reduce.9.cloned.1.call-start = ((), (), s32[]{:S(2)}) async-start(), calls=%async_computation.1 | async-start | bytes 819200 | tf_op jit(solution)/shard_map/psum | solution.py:147
  57.1 72.1 %all-reduce.11.cloned.1.call-start = ((), (), s32[]{:S(2)}) async-start(), calls=%async_computation.2 | async-start | bytes 819200 | tf_op jit(solution)/shard_map/psum | solution.py:178
  66.0 12.7 %copy-start.35 = (f32[512]{0:T(512)S(1)}, f32[512]{0:T(512)}, u32[]{:S(2)}) copy-start(f32[512]{0:T(512)} %param.30) | copy-start | bytes 6148
  81.5 3.6 copy-start.14
  93.6 2.9 copy-start.3
  109.4 239.9 %all-reduce.13.cloned.1.call-start = ((), (), s32[]{:S(2)}) async-start(), calls=%async_computation.3 | async-start | bytes 12582912 | tf_op jit(solution)/shard_map/psum | solution.py:196
  112.9 16.3 %copy-start.22 = (f32[196]{0:T(256)S(1)}, f32[196]{0:T(256)}, u32[]{:S(2)}) copy-start(f32[196]{0:T(256)} %copy-done.21) | copy-start | bytes 2356
  112.9 16.3 %copy-start.23 = (f32[512]{0:T(512)S(1)}, f32[512]{0:T(512)}, u32[]{:S(2)}) copy-start(f32[512]{0:T(512)} %param.18) | copy-start | bytes 6148
  112.9 16.3 %copy-start.25 = (f32[196]{0:T(256)S(1)}, f32[196]{0:T(256)}, u32[]{:S(2)}) copy-start(f32[196]{0:T(256)} %copy-done.24) | copy-start | bytes 2356
  112.9 17.6 %copy-start.29 = (f32[512]{0:T(512)S(1)}, f32[512]{0:T(512)}, u32[]{:S(2)}) copy-start(f32[512]{0:T(512)} %get-tuple-element.15) | copy-start | bytes 6148
  112.9 17.6 %copy-start.30 = (f32[512]{0:T(512)S(1)}, f32[512]{0:T(512)}, u32[]{:S(2)}) copy-start(f32[512]{0:T(512)} %get-tuple-element.21) | copy-start | bytes 6148
  112.9 17.6 %copy-start.31 = (f32[512]{0:T(512)S(1)}, f32[512]{0:T(512)}, u32[]{:S(2)}) copy-start(f32[512]{0:T(512)} %get-tuple-element.36) | copy-start | bytes 6148
  112.9 17.6 %copy-start.32 = (f32[512]{0:T(512)S(1)}, f32[512]{0:T(512)}, u32[]{:S(2)}) copy-start(f32[512]{0:T(512)} %get-tuple-element.45) | copy-start | bytes 6148
  112.9 17.6 %copy-start.34 = (f32[1024]{0:T(1024)S(1)}, f32[1024]{0:T(1024)}, u32[]{:S(2)}) copy-start(f32[1024]{0:T(1024)} %get-tuple-element.56) | copy-start | bytes 12292
  349.3 3.6 copy-start.5
  (16 other events, 26.2 us)
Sparse Core Ops, SparseCore 0:
  25.5 21.1 all-reduce.6
  57.2 19.6 all-reduce.8
  109.5 19.6 all-reduce.10
  136.6 212.6 all-reduce.12
